TPU v7x, 32 devices: a whole 2x2x4 slice. The times are simulated.
32 devices in a mesh: cuts: 2 (over core), lx: 2 (over x), ly: 8 (over z, y).
Axes of the slice: x: 2, y: 2, z: 4, core: 2. Of those that a mesh axis runs over, the one named last changes fastest.
Arguments:
- disorder: int32 [16, 16, 128], P('lx', 'ly'), may hold values from 0 to 255
- slice_bounds: float32 [12, 2], P('cuts'), may hold values from -1.5 to 1.5
- start: float32 [12, 32, 16, 16, 128], P('cuts', None, 'lx', 'ly'), may hold values from -36 to 36
- ritz: float32 [12, 8, 16, 16, 128], P('cuts', None, 'lx', 'ly'), may hold values from -4 to 4
Outputs:
- block: float32 [12, 32, 16, 16, 128], P('cuts', None, 'lx', 'ly')
- correlations: float32 [12, 16, 32], P('cuts')
All inputs are finite; a program needn't handle non-finite values.
Results may differ from a plain program's by a relative error of at most 0.000096.
Values sent between devices are 32-bit elements; how exact they have to be, the bound alone decides.
A program may use at most 64 MiB of HBM per device.

v0:
```python
import jax
import jax.numpy as jnp
from jax import lax
from jax.sharding import PartitionSpec as P

LEVELS = 256


def passed_along(value, axis, steps):
    count = lax.axis_size(axis)
    first, last = (max(0, -steps), min(count, count - steps))
    return lax.ppermute(value, axis, [(source, source + steps) for source in range(first, last)])


def padded_2(block, sides, width):
    for axis, dim in sides:
        count = lax.axis_size(axis)
        forward = [(i, i + 1) for i in range(count - 1)]
        forward.append((count - 1, 0))
        backward = [(target, source) for source, target in forward]
        low = lax.ppermute(
            lax.slice_in_dim(block, block.shape[dim] - width, None, axis=dim), axis, forward
        )
        high = lax.ppermute(lax.slice_in_dim(block, 0, width, axis=dim), axis, backward)
        block = jnp.concatenate([low, block, high], axis=dim)
    return block


def apply_scaled(field, onsite, centre):
    inner = field[:, 1:-1, 1:-1]
    beside = field[:, 2:, 1:-1] + field[:, :-2, 1:-1]
    beside = beside + field[:, 1:-1, 2:] + field[:, 1:-1, :-2]
    beside = beside + jnp.roll(inner, 1, 3) + jnp.roll(inner, -1, 3)
    return ((onsite[None] - centre) * inner - beside) / 16.0


def on_device(disorder, slice_bounds, start, ritz):
    onsite = 16.5 * (disorder.astype(jnp.float32) / jnp.float32(LEVELS - 1) - 0.5)
    count = start.shape[0]
    width = start.shape[1]
    centre = jnp.repeat((slice_bounds[:, 0] + slice_bounds[:, 1]) / 2.0, width)[:, None, None, None]
    vectors = start.reshape((count * width,) + start.shape[2:])
    lower_edge = passed_along(ritz[-1:], "cuts", 1)
    upper_edge = passed_along(ritz[:1], "cuts", -1)
    lower = jnp.concatenate([lower_edge, ritz[:-1]], 0)
    upper = jnp.concatenate([ritz[1:], upper_edge], 0)

    def filter_step(field):
        padded = padded_2(field, (("lx", 1), ("ly", 2)), 1)
        return apply_scaled(padded, onsite, centre)

    previous = vectors
    current = filter_step(vectors)
    previous, current = (current, 2.0 * filter_step(current) - previous)
    shape = current.shape
    cells = shape[1] * shape[2] * shape[3]
    total = jnp.float32(cells * lax.axis_size("lx") * lax.axis_size("ly"))
    hp = lax.Precision.HIGHEST
    filtered = current.reshape(count, width, cells)
    window = jnp.concatenate([lower, upper], 1).reshape(count, 2 * ritz.shape[1], cells)
    summed = lax.psum(jnp.einsum("src,svc->srv", window, filtered, precision=hp), ("lx", "ly"))
    correlation = summed / total
    cleaned = filtered - jnp.einsum("srv,src->svc", correlation, window, precision=hp)
    gram = lax.psum(jnp.einsum("sac,sbc->sab", cleaned, cleaned, precision=hp), ("lx", "ly"))
    factor = jnp.linalg.cholesky(gram / total)
    result = jax.scipy.linalg.solve_triangular(factor, cleaned, lower=True)
    return (result.reshape((count, width) + shape[1:]), correlation)


def solution(mesh):
    in_specs = (
        P("lx", "ly", None),
        P("cuts", None),
        P("cuts", None, "lx", "ly", None),
        P("cuts", None, "lx", "ly", None),
    )
    out_specs = (P("cuts", None, "lx", "ly", None), P("cuts", None, None))
    return jax.shard_map(
        on_device, mesh=mesh, in_specs=in_specs, out_specs=out_specs, check_vma=False
    )
```

profile of v0, /device:TPU:0, one launch (start us, length us, event | category | flops | bytes accessed | tf_op | source)
XLA Modules:
  0.0 334.0 jit_solution(6009458818156026938)
XLA Ops:
  1.7 3.0 collective-permute-start
  10.5 3.4 %collective-permute-done.1 = f32[192,1,2,128]{3,2,1,0:T(2,128)S(1)} collective-permute-done((f32[192,1,2,128]{3,2,1,0:T(2,128)S(1)}, f32[192,1,2,128]{3,2,1,0:T(2,128)S(1)}, u32[]{:S(2)}, u32[]{:S(2)}) %collective-permute-start.1) | collective-permute-done | bytes 196640 | tf_op jit(solution)/shard_map/ppermute | solution.py:21
  18.1 4.9 %collective-permute-start.2 = (f32[192,10,1,128]{3,2,1,0:T(1,128)S(1)}, f32[192,10,1,128]{3,2,1,0:T(1,128)}, u32[]{:S(2)}, u32[]{:S(2)}) collective-permute-start(f32[192,10,1,128]{3,2,1,0:T(1,128)S(1)} %get-tuple-element.4), channel_id=1, source_target_pairs={{1,0},{2,1},{3,2},{4,3},{5,4},{6,5},{7,6},{0,7},{9,8},{10,9},{11,1... | collective-permute-start | bytes 2949128 | tf_op jit(solution)/shard_map/ppermute | solution.py:24
  23.8 2.1 fusion.23
  26.0 2.1 fusion.24
  28.2 34.1 %collective-permute-done.2 = f32[192,10,1,128]{3,2,1,0:T(1,128)} collective-permute-done((f32[192,10,1,128]{3,2,1,0:T(1,128)S(1)}, f32[192,10,1,128]{3,2,1,0:T(1,128)}, u32[]{:S(2)}, u32[]{:S(2)}) %collective-permute-start.2) | collective-permute-done | bytes 983072 | tf_op jit(solution)/shard_map/ppermute | solution.py:24
  62.3 9.1 %fusion.1 = f32[192,8,2,128]{3,2,1,0:T(2,128)S(1)} fusion(f32[192,8,2,128]{3,2,1,0:T(2,128)S(1)} %bitcast.24, f32[192,10,1,128]{3,2,1,0:T(1,128)} %collective-permute-done.3, f32[192,1,2,128]{3,2,1,0:T(2,128)S(1)} %copy-done.4, f32[192,1,2,128]{3,2,1,0:T(2,128)S(1)} %copy-done.6, f32[192,10,1,128]{3,2,1,0:T(1,128)} %collective-permute-done.2, ...), kind=kLoop, calls=%fused_computation.6 | loop fusion | flops 7471104 | bytes 8659712 | tf_op jit(solution)/shard_map/div | solution.py:34
  73.8 5.6 %collective-permute-done.4 = f32[192,1,2,128]{3,2,1,0:T(2,128)S(1)} collective-permute-done((f32[192,1,2,128]{3,2,1,0:T(2,128)S(1)}, f32[192,1,2,128]{3,2,1,0:T(2,128)S(1)}, u32[]{:S(2)}, u32[]{:S(2)}) %collective-permute-start.4) | collective-permute-done | bytes 196640 | tf_op jit(solution)/shard_map/ppermute | solution.py:24
  79.3 3.0 collective-permute-done.5
  83.3 2.8 fusion.18
  86.1 2.8 collective-permute-start.6
  88.9 2.1 maximum_maximum_fusion
  91.0 2.6 reshape.34
  93.6 2.1 fusion.20
  95.8 2.1 fusion.21
  98.0 33.2 %collective-permute-done.6 = f32[192,10,1,128]{3,2,1,0:T(1,128)} collective-permute-done((f32[192,10,1,128]{3,2,1,0:T(1,128)}, f32[192,10,1,128]{3,2,1,0:T(1,128)}, u32[]{:S(2)}, u32[]{:S(2)}) %collective-permute-start.6) | collective-permute-done | bytes 983072 | tf_op jit(solution)/shard_map/ppermute | solution.py:24
  131.1 10.1 %fusion.4 = f32[192,8,2,128]{3,2,1,0:T(2,128)} fusion(f32[192,8,2,128]{3,2,1,0:T(2,128)S(1)} %fusion.1, f32[192,10,1,128]{3,2,1,0:T(1,128)} %collective-permute-done.7, f32[192,1,2,128]{3,2,1,0:T(2,128)S(1)} %collective-permute-done.4, f32[192,1,2,128]{3,2,1,0:T(2,128)S(1)} %collective-permute-done.5, f32[192,10,1,128]{3,2,1,0:T(1,128)} %collective-permute-done.6, ...), kind=kLoop, calls=%fused_computation.9 | loop fusion | flops 7864320 | bytes 10232576 | tf_op jit(solution)/shard_map/sub | solution.py:54
  141.2 2.6 reshape.33
  145.2 75.1 %psum.14 = f32[6,16,32]{2,1,0:T(8,128)S(1)} all-reduce(f32[6,16,32]{2,1,0:T(8,128)S(1)} %fusion.28), channel_id=1, replica_groups=mesh['cuts'=2,'lx'=2,'ly'=8] {'lx','ly'}, use_global_device_ids=true, to_apply=%region_0.1 | all-reduce | flops 3072 | bytes 24576 | tf_op jit(solution)/shard_map/psum | solution.py:61
  220.4 2.6 convolution_subtract_fusion
  224.5 72.8 %psum.15 = f32[6,32,32]{1,2,0:T(8,128)S(1)} all-reduce(f32[6,32,32]{1,2,0:T(8,128)S(1)} %fusion.29), channel_id=1, replica_groups=mesh['cuts'=2,'lx'=2,'ly'=8] {'lx','ly'}, use_global_device_ids=true, to_apply=%region_1.2 | all-reduce | flops 6144 | bytes 49152 | tf_op jit(solution)/shard_map/psum | solution.py:64
  297.4 17.6 %custom-call.8 = f32[6,32,32]{2,1,0:T(8,128)S(1)} custom-call(f32[6,32,32]{2,1,0:T(8,128)S(1)} %fusion.17), custom_call_target="Cholesky" | custom-call | tf_op jit(solution)/shard_map/jit(cholesky)/cholesky | solution.py:65
  315.2 14.8 %custom-call.9 = f32[6,1,32,32]{2,3,1,0:T(8,128)S(1)} custom-call(f32[6,1,32,32]{3,2,1,0:T(8,128)S(1)} %select_bitcast_fusion), custom_call_target="InvertDiagBlocksLowerTriangular" | custom-call | tf_op jit(solution)/shard_map/jit(_solve_triangular)/vmap()/triangular_solve | solution.py:66
  331.5 2.5 reshape.35
  (57 shorter events, 20.0 us)
Async XLA Ops:
  1.7 8.8 %collective-permute-start = (f32[192,1,2,128]{3,2,1,0:T(2,128)S(1)}, f32[192,1,2,128]{3,2,1,0:T(2,128)S(1)}, u32[]{:S(2)}, u32[]{:S(2)}) collective-permute-start(f32[192,1,2,128]{3,2,1,0:T(2,128)S(1)} %get-tuple-element.17), channel_id=1, source_target_pairs={{8,0},{0,8},{9,1},{1,9},{10,2},{2,10},{11,3},{3,11},{12,4},{4,12},... | collective-permute-start | bytes 589832 | tf_op jit(solution)/shard_map/ppermute | solution.py:24
  4.7 9.1 %collective-permute-start.1 = (f32[192,1,2,128]{3,2,1,0:T(2,128)S(1)}, f32[192,1,2,128]{3,2,1,0:T(2,128)S(1)}, u32[]{:S(2)}, u32[]{:S(2)}) collective-permute-start(f32[192,1,2,128]{3,2,1,0:T(2,128)S(1)} %get-tuple-element.16), channel_id=1, source_target_pairs={{0,8},{8,0},{1,9},{9,1},{2,10},{10,2},{3,11},{11,3},{4,12},{12,4},... | collective-permute-start | bytes 589832 | tf_op jit(solution)/shard_map/ppermute | solution.py:21
  6.3 82.5 %collective-permute-start.8 = (f32[1,8,8,2,128]{4,3,2,1,0:T(2,128)}, f32[1,8,8,2,128]{4,3,2,1,0:T(2,128)}, u32[]{:S(2)}, u32[]{:S(2)}) collective-permute-start(f32[1,8,8,2,128]{4,3,2,1,0:T(2,128)} %get-tuple-element.18), channel_id=1, source_target_pairs={{0,16},{1,17},{2,18},{3,19},{4,20},{5,21},{6,22},{7,23},{8,24},{9,... | collective-permute-start | bytes 196616 | tf_op jit(solution)/shard_map/ppermute | solution.py:12
  8.4 80.5 %collective-permute-start.9 = (f32[1,8,8,2,128]{4,3,2,1,0:T(2,128)}, f32[1,8,8,2,128]{4,3,2,1,0:T(2,128)}, u32[]{:S(2)}, u32[]{:S(2)}) collective-permute-start(f32[1,8,8,2,128]{4,3,2,1,0:T(2,128)} %get-tuple-element.19), channel_id=1, source_target_pairs={{16,0},{17,1},{18,2},{19,3},{20,4},{21,5},{22,6},{23,7},{24,8},{25... | collective-permute-start | bytes 196616 | tf_op jit(solution)/shard_map/ppermute | solution.py:12
  10.5 3.4 %copy-start.3 = (f32[192,1,2,128]{3,2,1,0:T(2,128)}, f32[192,1,2,128]{3,2,1,0:T(2,128)S(1)}, u32[]{:S(2)}) copy-start(f32[192,1,2,128]{3,2,1,0:T(2,128)S(1)} %collective-permute-done) | copy-start | bytes 589828
  13.8 0.7 copy-start.5
  16.5 6.4 %copy-start.10 = (f32[6,2]{0,1:T(2,128)S(1)}, f32[6,2]{0,1:T(2,128)}, u32[]{:S(2)}) copy-start(f32[6,2]{0,1:T(2,128)} %param.5) | copy-start | bytes 148
  16.6 7.3 %copy-start = (f32[6,32,8,2,128]{4,3,2,1,0:T(2,128)S(1)}, f32[6,32,8,2,128]{4,3,2,1,0:T(2,128)}, u32[]{:S(2)}) copy-start(f32[6,32,8,2,128]{4,3,2,1,0:T(2,128)} %param.6) | copy-start | bytes 4718596
  18.1 44.1 %collective-permute-start.2 = (f32[192,10,1,128]{3,2,1,0:T(1,128)S(1)}, f32[192,10,1,128]{3,2,1,0:T(1,128)}, u32[]{:S(2)}, u32[]{:S(2)}) collective-permute-start(f32[192,10,1,128]{3,2,1,0:T(1,128)S(1)} %get-tuple-element.4), channel_id=1, source_target_pairs={{1,0},{2,1},{3,2},{4,3},{5,4},{6,5},{7,6},{0,7},{9,8},{10,9},{11,1... | collective-permute-start | bytes 2949128 | tf_op jit(solution)/shard_map/ppermute | solution.py:24
  23.0 39.3 %collective-permute-start.3 = (f32[192,10,1,128]{3,2,1,0:T(1,128)S(1)}, f32[192,10,1,128]{3,2,1,0:T(1,128)}, u32[]{:S(2)}, u32[]{:S(2)}) collective-permute-start(f32[192,10,1,128]{3,2,1,0:T(1,128)S(1)} %get-tuple-element.5), channel_id=1, source_target_pairs={{0,1},{1,2},{2,3},{3,4},{4,5},{5,6},{6,7},{7,0},{8,9},{9,10},{10,1... | collective-permute-start | bytes 2949128 | tf_op jit(solution)/shard_map/ppermute | solution.py:21
  23.1 39.1 %copy-start.8 = (f32[192]{0:T(256)}, f32[192]{0:T(256)S(1)}, u32[]{:S(2)}) copy-start(f32[192]{0:T(256)S(1)} %sub.40) | copy-start | bytes 2308
  26.0 36.3 %copy-start.4 = (f32[192,1,2,128]{3,2,1,0:T(2,128)S(1)}, f32[192,1,2,128]{3,2,1,0:T(2,128)}, u32[]{:S(2)}) copy-start(f32[192,1,2,128]{3,2,1,0:T(2,128)} %copy-done.3) | copy-start | bytes 589828
  26.0 36.3 %copy-start.6 = (f32[192,1,2,128]{3,2,1,0:T(2,128)S(1)}, f32[192,1,2,128]{3,2,1,0:T(2,128)}, u32[]{:S(2)}) copy-start(f32[192,1,2,128]{3,2,1,0:T(2,128)} %copy-done.5) | copy-start | bytes 589828
  62.3 11.3 %copy-start.2 = (f32[6,8,8,2,128]{4,3,2,1,0:T(2,128)S(1)}, f32[6,8,8,2,128]{4,3,2,1,0:T(2,128)}, u32[]{:S(2)}) copy-start(f32[6,8,8,2,128]{4,3,2,1,0:T(2,128)} %param.7) | copy-start | bytes 1179652
  71.5 7.8 %collective-permute-start.4 = (f32[192,1,2,128]{3,2,1,0:T(2,128)S(1)}, f32[192,1,2,128]{3,2,1,0:T(2,128)S(1)}, u32[]{:S(2)}, u32[]{:S(2)}) collective-permute-start(f32[192,1,2,128]{3,2,1,0:T(2,128)S(1)} %get-tuple-element.11), channel_id=1, source_target_pairs={{8,0},{0,8},{9,1},{1,9},{10,2},{2,10},{11,3},{3,11},{12,4},{4,12},... | collective-permute-start | bytes 589832 | tf_op jit(solution)/shard_map/ppermute | solution.py:24
  73.0 9.4 %collective-permute-start.5 = (f32[192,1,2,128]{3,2,1,0:T(2,128)S(1)}, f32[192,1,2,128]{3,2,1,0:T(2,128)S(1)}, u32[]{:S(2)}, u32[]{:S(2)}) collective-permute-start(f32[192,1,2,128]{3,2,1,0:T(2,128)S(1)} %get-tuple-element.10), channel_id=1, source_target_pairs={{0,8},{8,0},{1,9},{9,1},{2,10},{10,2},{3,11},{11,3},{4,12},{12,4},... | collective-permute-start | bytes 589832 | tf_op jit(solution)/shard_map/ppermute | solution.py:21
  86.1 45.1 %collective-permute-start.6 = (f32[192,10,1,128]{3,2,1,0:T(1,128)}, f32[192,10,1,128]{3,2,1,0:T(1,128)}, u32[]{:S(2)}, u32[]{:S(2)}) collective-permute-start(f32[192,10,1,128]{3,2,1,0:T(1,128)} %get-tuple-element.2), channel_id=1, source_target_pairs={{1,0},{2,1},{3,2},{4,3},{5,4},{6,5},{7,6},{0,7},{9,8},{10,9},{11,1... | collective-permute-start | bytes 2949128 | tf_op jit(solution)/shard_map/ppermute | solution.py:24
  88.9 42.3 %collective-permute-start.7 = (f32[192,10,1,128]{3,2,1,0:T(1,128)}, f32[192,10,1,128]{3,2,1,0:T(1,128)}, u32[]{:S(2)}, u32[]{:S(2)}) collective-permute-start(f32[192,10,1,128]{3,2,1,0:T(1,128)} %get-tuple-element.3), channel_id=1, source_target_pairs={{0,1},{1,2},{2,3},{3,4},{4,5},{5,6},{6,7},{7,0},{8,9},{9,10},{10,1... | collective-permute-start | bytes 2949128 | tf_op jit(solution)/shard_map/ppermute | solution.py:21
  95.8 35.3 %copy-start.9 = (f32[192]{0:T(256)S(1)}, f32[192]{0:T(256)}, u32[]{:S(2)}) copy-start(f32[192]{0:T(256)} %copy-done.8) | copy-start | bytes 2308
  141.2 2.6 copy-start.1
  220.3 2.6 copy-start.7
where the time goes:
time: 335 us; the launch traced here: 334 us
  blocking collectives  148 us (44%)
  waiting for transfers between devices  80 us (24%)
  other arithmetic  57.5 us (17%)
  local copies, waits for them, and re-layouts  24.5 us (7%)
  starting transfers between devices  16.2 us (5%)
  matrix products  6.98 us (2%)
    psum x1, blocking collectives, on_device(): lax.psum(jnp.einsum('src,svc->srv', window, filtered, precision=hp), ('lx...  75.1 us
    ppermute x4, waiting for transfers between devices, padded_2(): lax.ppermute(lax.slice_in_dim(block, 0, width, axis=dim), axis, backward)  73.6 us
    psum x1, blocking collectives, on_device(): lax.psum(jnp.einsum('sac,sbc->sab', cleaned, cleaned, precision=hp), ('lx...  72.8 us
    another operation x4, other arithmetic, on_device(): factor = jnp.linalg.cholesky(gram / total)  17.7 us
    another operation x3, other arithmetic, on_device(): result = jax.scipy.linalg.solve_triangular(factor, cleaned, lower=True)  14.9 us
    ppermute x4, starting transfers between devices, padded_2(): lax.ppermute(lax.slice_in_dim(block, 0, width, axis=dim), axis, backward)  12.2 us
    sub x1, other arithmetic, on_device(): previous, current = (current, 2.0 * filter_step(current) - previous)  10.1 us
    div x1, other arithmetic, apply_scaled(): return ((onsite[None] - centre) * inner - beside) / 16.0  9.07 us
  transfers between devices with their start and end apart: 10, of which 6 were waited for; matrix products, arithmetic and copies ran while one was open for 10% of the time, Pallas kernels for 0%

commit v1 on v0

--- a/solution.py
+++ b/solution.py
@@ -58,7 +58,9 @@
     hp = lax.Precision.HIGHEST
     filtered = current.reshape(count, width, cells)
     window = jnp.concatenate([lower, upper], 1).reshape(count, 2 * ritz.shape[1], cells)
-    summed = lax.psum(jnp.einsum("src,svc->srv", window, filtered, precision=hp), ("lx", "ly"))
+    summed = lax.psum(
+        lax.psum(jnp.einsum("src,svc->srv", window, filtered, precision=hp), "ly"), "lx"
+    )
     correlation = summed / total
     cleaned = filtered - jnp.einsum("srv,src->svc", correlation, window, precision=hp)
     gram = lax.psum(jnp.einsum("sac,sbc->sab", cleaned, cleaned, precision=hp), ("lx", "ly"))

time: 335 us -> 304 us (0.907)
  blocking collectives: 148 us -> 117 us
    psum x1 -> x2, blocking collectives: 75.1 us -> 44.6 us  [the longest x1 35.8 us: on_device(): lax.psum(jnp.einsum('src,svc->srv', window, filtered, precision=hp), 'ly')]
  transfers between devices with their start and end apart: 10 -> 10, of which waited for: 6 -> 6; matrix products, arithmetic and copies ran while one was open for 10% -> 11% of each run, Pallas kernels for 0% -> 0%
where the time goes in v1:
time: 304 us; the launch traced here: 303 us
  blocking collectives  117 us (38%)
  waiting for transfers between devices  80 us (26%)
  other arithmetic  57.5 us (19%)
  local copies, waits for them, and re-layouts  24.5 us (8%)
  starting transfers between devices  16.2 us (5%)
  matrix products  6.98 us (2%)
    ppermute x4, waiting for transfers between devices, padded_2(): lax.ppermute(lax.slice_in_dim(block, 0, width, axis=dim), axis, backward)  73.6 us
    psum x1, blocking collectives, on_device(): lax.psum(jnp.einsum('sac,sbc->sab', cleaned, cleaned, precision=hp), ('lx...  72.5 us
    psum x1, blocking collectives, on_device(): lax.psum(jnp.einsum('src,svc->srv', window, filtered, precision=hp), 'ly')  35.8 us
    another operation x4, other arithmetic, on_device(): factor = jnp.linalg.cholesky(gram / total)  17.7 us
    another operation x3, other arithmetic, on_device(): result = jax.scipy.linalg.solve_triangular(factor, cleaned, lower=True)  14.9 us
    ppermute x4, starting transfers between devices, padded_2(): lax.ppermute(lax.slice_in_dim(block, 0, width, axis=dim), axis, backward)  12.2 us
    sub x1, other arithmetic, on_device(): previous, current = (current, 2.0 * filter_step(current) - previous)  10.1 us
    div x1, other arithmetic, apply_scaled(): return ((onsite[None] - centre) * inner - beside) / 16.0  9.07 us
  transfers between devices with their start and end apart: 10, of which 6 were waited for; matrix products, arithmetic and copies ran while one was open for 11% of the time, Pallas kernels for 0%

profile of v1, /device:TPU:0, one launch (start us, length us, event | category | flops | bytes accessed | tf_op | source)
XLA Modules:
  0.0 303.2 jit_solution(9700470494834097760)
XLA Ops:
  1.7 3.0 collective-permute-start
  10.5 3.4 %collective-permute-done.1 = f32[192,1,2,128]{3,2,1,0:T(2,128)S(1)} collective-permute-done((f32[192,1,2,128]{3,2,1,0:T(2,128)S(1)}, f32[192,1,2,128]{3,2,1,0:T(2,128)S(1)}, u32[]{:S(2)}, u32[]{:S(2)}) %collective-permute-start.1) | collective-permute-done | bytes 196640 | tf_op jit(solution)/shard_map/ppermute | solution.py:21
  18.1 4.9 %collective-permute-start.2 = (f32[192,10,1,128]{3,2,1,0:T(1,128)S(1)}, f32[192,10,1,128]{3,2,1,0:T(1,128)}, u32[]{:S(2)}, u32[]{:S(2)}) collective-permute-start(f32[192,10,1,128]{3,2,1,0:T(1,128)S(1)} %get-tuple-element.4), channel_id=1, source_target_pairs={{1,0},{2,1},{3,2},{4,3},{5,4},{6,5},{7,6},{0,7},{9,8},{10,9},{11,1... | collective-permute-start | bytes 2949128 | tf_op jit(solution)/shard_map/ppermute | solution.py:24
  23.8 2.1 fusion.23
  26.0 2.1 fusion.24
  28.2 34.1 %collective-permute-done.2 = f32[192,10,1,128]{3,2,1,0:T(1,128)} collective-permute-done((f32[192,10,1,128]{3,2,1,0:T(1,128)S(1)}, f32[192,10,1,128]{3,2,1,0:T(1,128)}, u32[]{:S(2)}, u32[]{:S(2)}) %collective-permute-start.2) | collective-permute-done | bytes 983072 | tf_op jit(solution)/shard_map/ppermute | solution.py:24
  62.3 9.1 %fusion.1 = f32[192,8,2,128]{3,2,1,0:T(2,128)S(1)} fusion(f32[192,8,2,128]{3,2,1,0:T(2,128)S(1)} %bitcast.24, f32[192,10,1,128]{3,2,1,0:T(1,128)} %collective-permute-done.3, f32[192,1,2,128]{3,2,1,0:T(2,128)S(1)} %copy-done.4, f32[192,1,2,128]{3,2,1,0:T(2,128)S(1)} %copy-done.6, f32[192,10,1,128]{3,2,1,0:T(1,128)} %collective-permute-done.2, ...), kind=kLoop, calls=%fused_computation.6 | loop fusion | flops 7471104 | bytes 8659712 | tf_op jit(solution)/shard_map/div | solution.py:34
  73.8 5.6 %collective-permute-done.4 = f32[192,1,2,128]{3,2,1,0:T(2,128)S(1)} collective-permute-done((f32[192,1,2,128]{3,2,1,0:T(2,128)S(1)}, f32[192,1,2,128]{3,2,1,0:T(2,128)S(1)}, u32[]{:S(2)}, u32[]{:S(2)}) %collective-permute-start.4) | collective-permute-done | bytes 196640 | tf_op jit(solution)/shard_map/ppermute | solution.py:24
  79.3 3.0 %collective-permute-done.5 = f32[192,1,2,128]{3,2,1,0:T(2,128)S(1)} collective-permute-done((f32[192,1,2,128]{3,2,1,0:T(2,128)S(1)}, f32[192,1,2,128]{3,2,1,0:T(2,128)S(1)}, u32[]{:S(2)}, u32[]{:S(2)}) %collective-permute-start.5) | collective-permute-done | bytes 196640 | tf_op jit(solution)/shard_map/ppermute | solution.py:21
  83.3 2.8 fusion.18
  86.1 2.8 collective-permute-start.6
  91.0 2.6 reshape.34
  93.6 2.1 fusion.20
  95.8 2.1 fusion.21
  98.0 33.2 %collective-permute-done.6 = f32[192,10,1,128]{3,2,1,0:T(1,128)} collective-permute-done((f32[192,10,1,128]{3,2,1,0:T(1,128)}, f32[192,10,1,128]{3,2,1,0:T(1,128)}, u32[]{:S(2)}, u32[]{:S(2)}) %collective-permute-start.6) | collective-permute-done | bytes 983072 | tf_op jit(solution)/shard_map/ppermute | solution.py:24
  131.1 10.1 %fusion.4 = f32[192,8,2,128]{3,2,1,0:T(2,128)} fusion(f32[192,8,2,128]{3,2,1,0:T(2,128)S(1)} %fusion.1, f32[192,10,1,128]{3,2,1,0:T(1,128)} %collective-permute-done.7, f32[192,1,2,128]{3,2,1,0:T(2,128)S(1)} %collective-permute-done.4, f32[192,1,2,128]{3,2,1,0:T(2,128)S(1)} %collective-permute-done.5, f32[192,10,1,128]{3,2,1,0:T(1,128)} %collective-permute-done.6, ...), kind=kLoop, calls=%fused_computation.9 | loop fusion | flops 7864320 | bytes 10232576 | tf_op jit(solution)/shard_map/sub | solution.py:54
  141.2 2.6 reshape.33
  145.2 35.8 %psum.21 = f32[6,16,32]{2,1,0:T(8,128)S(1)} all-reduce(f32[6,16,32]{2,1,0:T(8,128)S(1)} %fusion.28), channel_id=1, replica_groups=mesh['cuts'=2,'lx'=2,'ly'=8] {'ly'}, use_global_device_ids=true, to_apply=%region_0.1 | all-reduce | flops 3072 | bytes 24576 | tf_op jit(solution)/shard_map/psum | solution.py:62
  181.0 8.8 %psum.22 = f32[6,16,32]{2,1,0:T(8,128)S(1)} all-reduce(f32[6,16,32]{2,1,0:T(8,128)S(1)} %psum.21), channel_id=1, replica_groups=mesh['cuts'=2,'lx'=2,'ly'=8] {'lx'}, use_global_device_ids=true, to_apply=%region_1.2 | all-reduce | flops 3072 | bytes 24576 | tf_op jit(solution)/shard_map/psum | solution.py:61
  189.9 2.6 convolution_subtract_fusion
  194.0 72.5 %psum.23 = f32[6,32,32]{1,2,0:T(8,128)S(1)} all-reduce(f32[6,32,32]{1,2,0:T(8,128)S(1)} %fusion.29), channel_id=1, replica_groups=mesh['cuts'=2,'lx'=2,'ly'=8] {'lx','ly'}, use_global_device_ids=true, to_apply=%region_2.3 | all-reduce | flops 6144 | bytes 49152 | tf_op jit(solution)/shard_map/psum | solution.py:66
  266.6 17.6 %custom-call.8 = f32[6,32,32]{2,1,0:T(8,128)S(1)} custom-call(f32[6,32,32]{2,1,0:T(8,128)S(1)} %fusion.17), custom_call_target="Cholesky" | custom-call | tf_op jit(solution)/shard_map/jit(cholesky)/cholesky | solution.py:67
  284.4 14.8 %custom-call.9 = f32[6,1,32,32]{2,3,1,0:T(8,128)S(1)} custom-call(f32[6,1,32,32]{3,2,1,0:T(8,128)S(1)} %select_bitcast_fusion), custom_call_target="InvertDiagBlocksLowerTriangular" | custom-call | tf_op jit(solution)/shard_map/jit(_solve_triangular)/vmap()/triangular_solve | solution.py:68
  300.7 2.5 reshape.35
  (58 shorter events, 22.1 us)
Async XLA Ops:
  1.7 8.8 %collective-permute-start = (f32[192,1,2,128]{3,2,1,0:T(2,128)S(1)}, f32[192,1,2,128]{3,2,1,0:T(2,128)S(1)}, u32[]{:S(2)}, u32[]{:S(2)}) collective-permute-start(f32[192,1,2,128]{3,2,1,0:T(2,128)S(1)} %get-tuple-element.17), channel_id=1, source_target_pairs={{8,0},{0,8},{9,1},{1,9},{10,2},{2,10},{11,3},{3,11},{12,4},{4,12},... | collective-permute-start | bytes 589832 | tf_op jit(solution)/shard_map/ppermute | solution.py:24
  4.7 9.1 %collective-permute-start.1 = (f32[192,1,2,128]{3,2,1,0:T(2,128)S(1)}, f32[192,1,2,128]{3,2,1,0:T(2,128)S(1)}, u32[]{:S(2)}, u32[]{:S(2)}) collective-permute-start(f32[192,1,2,128]{3,2,1,0:T(2,128)S(1)} %get-tuple-element.16), channel_id=1, source_target_pairs={{0,8},{8,0},{1,9},{9,1},{2,10},{10,2},{3,11},{11,3},{4,12},{12,4},... | collective-permute-start | bytes 589832 | tf_op jit(solution)/shard_map/ppermute | solution.py:21
  6.3 82.5 %collective-permute-start.8 = (f32[1,8,8,2,128]{4,3,2,1,0:T(2,128)}, f32[1,8,8,2,128]{4,3,2,1,0:T(2,128)}, u32[]{:S(2)}, u32[]{:S(2)}) collective-permute-start(f32[1,8,8,2,128]{4,3,2,1,0:T(2,128)} %get-tuple-element.18), channel_id=1, source_target_pairs={{0,16},{1,17},{2,18},{3,19},{4,20},{5,21},{6,22},{7,23},{8,24},{9,... | collective-permute-start | bytes 196616 | tf_op jit(solution)/shard_map/ppermute | solution.py:12
  8.4 80.5 %collective-permute-start.9 = (f32[1,8,8,2,128]{4,3,2,1,0:T(2,128)}, f32[1,8,8,2,128]{4,3,2,1,0:T(2,128)}, u32[]{:S(2)}, u32[]{:S(2)}) collective-permute-start(f32[1,8,8,2,128]{4,3,2,1,0:T(2,128)} %get-tuple-element.19), channel_id=1, source_target_pairs={{16,0},{17,1},{18,2},{19,3},{20,4},{21,5},{22,6},{23,7},{24,8},{25... | collective-permute-start | bytes 196616 | tf_op jit(solution)/shard_map/ppermute | solution.py:12
  10.5 3.4 %copy-start.3 = (f32[192,1,2,128]{3,2,1,0:T(2,128)}, f32[192,1,2,128]{3,2,1,0:T(2,128)S(1)}, u32[]{:S(2)}) copy-start(f32[192,1,2,128]{3,2,1,0:T(2,128)S(1)} %collective-permute-done) | copy-start | bytes 589828
  13.8 0.7 copy-start.5
  16.5 6.4 %copy-start.10 = (f32[6,2]{0,1:T(2,128)S(1)}, f32[6,2]{0,1:T(2,128)}, u32[]{:S(2)}) copy-start(f32[6,2]{0,1:T(2,128)} %param.5) | copy-start | bytes 148
  16.6 7.3 %copy-start = (f32[6,32,8,2,128]{4,3,2,1,0:T(2,128)S(1)}, f32[6,32,8,2,128]{4,3,2,1,0:T(2,128)}, u32[]{:S(2)}) copy-start(f32[6,32,8,2,128]{4,3,2,1,0:T(2,128)} %param.6) | copy-start | bytes 4718596
  18.1 44.1 %collective-permute-start.2 = (f32[192,10,1,128]{3,2,1,0:T(1,128)S(1)}, f32[192,10,1,128]{3,2,1,0:T(1,128)}, u32[]{:S(2)}, u32[]{:S(2)}) collective-permute-start(f32[192,10,1,128]{3,2,1,0:T(1,128)S(1)} %get-tuple-element.4), channel_id=1, source_target_pairs={{1,0},{2,1},{3,2},{4,3},{5,4},{6,5},{7,6},{0,7},{9,8},{10,9},{11,1... | collective-permute-start | bytes 2949128 | tf_op jit(solution)/shard_map/ppermute | solution.py:24
  23.0 39.3 %collective-permute-start.3 = (f32[192,10,1,128]{3,2,1,0:T(1,128)S(1)}, f32[192,10,1,128]{3,2,1,0:T(1,128)}, u32[]{:S(2)}, u32[]{:S(2)}) collective-permute-start(f32[192,10,1,128]{3,2,1,0:T(1,128)S(1)} %get-tuple-element.5), channel_id=1, source_target_pairs={{0,1},{1,2},{2,3},{3,4},{4,5},{5,6},{6,7},{7,0},{8,9},{9,10},{10,1... | collective-permute-start | bytes 2949128 | tf_op jit(solution)/shard_map/ppermute | solution.py:21
  23.1 39.1 %copy-start.8 = (f32[192]{0:T(256)}, f32[192]{0:T(256)S(1)}, u32[]{:S(2)}) copy-start(f32[192]{0:T(256)S(1)} %sub.40) | copy-start | bytes 2308
  26.0 36.3 %copy-start.4 = (f32[192,1,2,128]{3,2,1,0:T(2,128)S(1)}, f32[192,1,2,128]{3,2,1,0:T(2,128)}, u32[]{:S(2)}) copy-start(f32[192,1,2,128]{3,2,1,0:T(2,128)} %copy-done.3) | copy-start | bytes 589828
  26.0 36.3 %copy-start.6 = (f32[192,1,2,128]{3,2,1,0:T(2,128)S(1)}, f32[192,1,2,128]{3,2,1,0:T(2,128)}, u32[]{:S(2)}) copy-start(f32[192,1,2,128]{3,2,1,0:T(2,128)} %copy-done.5) | copy-start | bytes 589828
  62.3 11.3 %copy-start.2 = (f32[6,8,8,2,128]{4,3,2,1,0:T(2,128)S(1)}, f32[6,8,8,2,128]{4,3,2,1,0:T(2,128)}, u32[]{:S(2)}) copy-start(f32[6,8,8,2,128]{4,3,2,1,0:T(2,128)} %param.7) | copy-start | bytes 1179652
  71.5 7.8 %collective-permute-start.4 = (f32[192,1,2,128]{3,2,1,0:T(2,128)S(1)}, f32[192,1,2,128]{3,2,1,0:T(2,128)S(1)}, u32[]{:S(2)}, u32[]{:S(2)}) collective-permute-start(f32[192,1,2,128]{3,2,1,0:T(2,128)S(1)} %get-tuple-element.11), channel_id=1, source_target_pairs={{8,0},{0,8},{9,1},{1,9},{10,2},{2,10},{11,3},{3,11},{12,4},{4,12},... | collective-permute-start | bytes 589832 | tf_op jit(solution)/shard_map/ppermute | solution.py:24
  73.0 9.4 %collective-permute-start.5 = (f32[192,1,2,128]{3,2,1,0:T(2,128)S(1)}, f32[192,1,2,128]{3,2,1,0:T(2,128)S(1)}, u32[]{:S(2)}, u32[]{:S(2)}) collective-permute-start(f32[192,1,2,128]{3,2,1,0:T(2,128)S(1)} %get-tuple-element.10), channel_id=1, source_target_pairs={{0,8},{8,0},{1,9},{9,1},{2,10},{10,2},{3,11},{11,3},{4,12},{12,4},... | collective-permute-start | bytes 589832 | tf_op jit(solution)/shard_map/ppermute | solution.py:21
  86.1 45.1 %collective-permute-start.6 = (f32[192,10,1,128]{3,2,1,0:T(1,128)}, f32[192,10,1,128]{3,2,1,0:T(1,128)}, u32[]{:S(2)}, u32[]{:S(2)}) collective-permute-start(f32[192,10,1,128]{3,2,1,0:T(1,128)} %get-tuple-element.2), channel_id=1, source_target_pairs={{1,0},{2,1},{3,2},{4,3},{5,4},{6,5},{7,6},{0,7},{9,8},{10,9},{11,1... | collective-permute-start | bytes 2949128 | tf_op jit(solution)/shard_map/ppermute | solution.py:24
  88.9 42.3 %collective-permute-start.7 = (f32[192,10,1,128]{3,2,1,0:T(1,128)}, f32[192,10,1,128]{3,2,1,0:T(1,128)}, u32[]{:S(2)}, u32[]{:S(2)}) collective-permute-start(f32[192,10,1,128]{3,2,1,0:T(1,128)} %get-tuple-element.3), channel_id=1, source_target_pairs={{0,1},{1,2},{2,3},{3,4},{4,5},{5,6},{6,7},{7,0},{8,9},{9,10},{10,1... | collective-permute-start | bytes 2949128 | tf_op jit(solution)/shard_map/ppermute | solution.py:21
  95.8 35.3 %copy-start.9 = (f32[192]{0:T(256)S(1)}, f32[192]{0:T(256)}, u32[]{:S(2)}) copy-start(f32[192]{0:T(256)} %copy-done.8) | copy-start | bytes 2308
  141.2 2.6 copy-start.1
  189.8 2.6 copy-start.7
